TPU v7x, 32 devices: a whole 2x2x4 slice. The times are simulated.
32 devices in a mesh: dp: 8 (over z, core), mp: 4 (over y, x).
Axes of the slice: x: 2, y: 2, z: 4, core: 2. Of those that a mesh axis runs over, the one named last changes fastest.
Arguments:
- tokens: bfloat16 [2048, 3072], P('dp'), may hold values from -60 to 60
- ln_gain: float32 [3072], replicated, may hold values from 0.25 to 1.75
- q_weight: bfloat16 [3072, 4096], P('dp', 'mp'), may hold values from -1 to 1
- k_weight: bfloat16 [3072, 4096], P('dp', 'mp'), may hold values from -1 to 1
- v_weight: bfloat16 [3072, 4096], P('dp', 'mp'), may hold values from -0.109375 to 0.109375
- q_gain: float32 [4096], P('mp'), may hold values from 0.6 to 6
- k_gain: float32 [4096], P('mp'), may hold values from 0.6 to 6
- out_weight: bfloat16 [3072, 4096], P('dp', 'mp'), may hold values from -0.25 to 0.25
Outputs:
- mixed: bfloat16 [2048, 3072], P(('dp', 'mp'))
All inputs are finite; a program needn't handle non-finite values.
Results may differ from a plain program's by a relative error of at most 0.018.
Values may be sent and summed in bfloat16 or wider, within the bound.
A program may use at most 128 MiB of HBM per device.

v0:
```python
import math

import jax
import jax.numpy as jnp
from jax import lax
from jax.sharding import PartitionSpec as P

HEAD_DIM = 128
IMG_TOKENS = 256


epsilon = 1e-06


def layer_norm(values, scale_gain):
    average = jnp.mean(values, axis=-1, keepdims=True)
    centred = values - average
    variance = jnp.mean(centred * centred, axis=-1, keepdims=True)
    return centred * lax.rsqrt(variance + epsilon) * scale_gain


def head_norm(projected, scale_gain):
    heads_count = projected.shape[1] // HEAD_DIM
    shaped = projected.reshape(projected.shape[0], heads_count, HEAD_DIM)
    normed = layer_norm(shaped, scale_gain.reshape(heads_count, HEAD_DIM))
    return normed.reshape(projected.shape).astype(jnp.bfloat16)


def attend(queries, key_rows, value_rows):
    scores = jnp.einsum(
        "bqhd,bkhd->bhqk", queries, key_rows, preferred_element_type=jnp.float32
    ) * (1.0 / math.sqrt(HEAD_DIM))
    highest = jnp.max(scores, axis=-1, keepdims=True)
    weights = jnp.exp(scores - highest)
    probs = (weights / jnp.sum(weights, axis=-1, keepdims=True)).astype(jnp.bfloat16)
    context = jnp.einsum("bhqk,bkhd->bqhd", probs, value_rows, preferred_element_type=jnp.float32)
    return context.astype(jnp.bfloat16)


def place_three(holder, pieces, offset, local_width):
    holder = lax.dynamic_update_slice(holder, pieces[0], (offset, 0))
    holder = lax.dynamic_update_slice(holder, pieces[1], (offset, local_width))
    return lax.dynamic_update_slice(holder, pieces[2], (offset, 2 * local_width))


def on_device(tokens, ln_gain, q_weight, k_weight, v_weight, q_gain, k_gain, out_weight):
    normed = layer_norm(tokens.astype(jnp.float32), ln_gain).astype(jnp.bfloat16)
    token_count = normed.shape[0]
    local_width = q_weight.shape[1]
    feature_count = normed.shape[1]
    stacked = jnp.zeros((feature_count, 3 * local_width), jnp.bfloat16)
    projections = place_three(
        stacked,
        (
            lax.all_gather(q_weight, "dp", axis=0, tiled=True),
            lax.all_gather(k_weight, "dp", axis=0, tiled=True),
            lax.all_gather(v_weight, "dp", axis=0, tiled=True),
        ),
        jnp.int32(0),
        local_width,
    )
    combined = jnp.dot(normed, projections, preferred_element_type=jnp.float32)
    queries = combined[:, :local_width]
    key_rows = combined[:, local_width : 2 * local_width]
    value_cast = combined[:, 2 * local_width :].astype(jnp.bfloat16)
    query_normed = head_norm(queries, q_gain)
    key_normed = head_norm(key_rows, k_gain)
    images = token_count // IMG_TOKENS
    shaped = (images, IMG_TOKENS, local_width // HEAD_DIM, HEAD_DIM)
    context = attend(
        query_normed.reshape(shaped), key_normed.reshape(shaped), value_cast.reshape(shaped)
    )
    context = context.reshape(token_count, local_width)
    out_full = lax.all_gather(out_weight, "dp", axis=0, tiled=True)
    return lax.psum_scatter(
        lax.dot_general(
            context, out_full, (((1,), (1,)), ((), ())), preferred_element_type=jnp.float32
        ).astype(jnp.bfloat16),
        "mp",
        scatter_dimension=0,
        tiled=True,
    )


def solution(mesh):
    in_specs = (
        P("dp", None),
        P(),
        P("dp", "mp"),
        P("dp", "mp"),
        P("dp", "mp"),
        P("mp"),
        P("mp"),
        P("dp", "mp"),
    )
    out_specs = P(("dp", "mp"), None)
    return jax.shard_map(
        on_device, mesh=mesh, in_specs=in_specs, out_specs=out_specs, check_vma=False
    )
```

profile of v0, /device:TPU:0, one launch (start us, length us, event | category | flops | bytes accessed | tf_op | source)
XLA Modules:
  0.0 313.6 jit_solution(10652780476006178973)
XLA Ops:
  6.5 0.0 copy-start.2
  6.5 0.0 all-gather.5.cloned.1.call-start
  6.5 0.7 all-gather.5.cloned.1.call-update
  7.3 0.0 all-gather.7.cloned.1.call-start
  7.3 0.7 all-gather.7.cloned.1.call-update
  8.0 0.0 all-gather.9.cloned.1.call-start
  8.1 0.7 all-gather.9.cloned.1.call-update
  8.7 0.0 all-gather.11.cloned.1.call-start
  8.8 0.5 all-gather.11.cloned.1.call-update
  9.3 0.0 reduce-scatter.2.cloned.1.call-start
  9.4 0.0 copy-done.2
  9.4 0.3 convert_reduce_fusion
  9.7 0.6 fusion.3
  10.2 66.2 %all-gather.5.cloned.1.call-done = bf16[3072,1024]{1,0:T(8,128)(2,1)} async-done(((bf16[384,1024]{1,0:T(8,128)(2,1)}), bf16[3072,1024]{1,0:T(8,128)(2,1)}) %all-gather.5.cloned.1.call-update) | async-done | bytes 6291472 | tf_op jit(solution)/shard_map/all_gather | solution.py:55
  76.4 9.7 %dynamic_update_slice.9 = bf16[3072,3072]{1,0:T(8,128)(2,1)} pad(bf16[3072,1024]{1,0:T(8,128)(2,1)} %all-gather.5.cloned.1.call-done, bf16[]{:T(256)} %constant.8.clone.1), padding=0_0x0_2048 | pad | bytes 25165826 | tf_op jit(solution)/shard_map/dynamic_update_slice | solution.py:41
  86.1 55.3 %all-gather.7.cloned.1.call-done = bf16[3072,1024]{1,0:T(8,128)(2,1)} async-done(((bf16[384,1024]{1,0:T(8,128)(2,1)}), bf16[3072,1024]{1,0:T(8,128)(2,1)}) %all-gather.7.cloned.1.call-update) | async-done | bytes 6291472 | tf_op jit(solution)/shard_map/all_gather | solution.py:56
  141.4 6.3 %constant_dynamic-update-slice_fusion.1 = bf16[3072,3072]{1,0:T(8,128)(2,1)} fusion(bf16[3072,3072]{1,0:T(8,128)(2,1)} %dynamic_update_slice.9, bf16[3072,1024]{1,0:T(8,128)(2,1)} %all-gather.7.cloned.1.call-done), kind=kLoop, calls=%fused_computation.45 | loop fusion | bytes 12582912 | tf_op jit(solution)/shard_map/dynamic_update_slice | solution.py:42
  147.8 0.0 copy-start.7
  147.8 58.7 %all-gather.9.cloned.1.call-done = bf16[3072,1024]{1,0:T(8,128)(2,1)} async-done(((bf16[384,1024]{1,0:T(8,128)(2,1)}), bf16[3072,1024]{1,0:T(8,128)(2,1)}) %all-gather.9.cloned.1.call-update) | async-done | bytes 6291472 | tf_op jit(solution)/shard_map/all_gather | solution.py:57
  206.5 0.0 copy-start.3
  206.5 6.3 %constant_dynamic-update-slice_fusion = bf16[3072,3072]{1,0:T(8,128)(2,1)} fusion(bf16[3072,3072]{1,0:T(8,128)(2,1)} %constant_dynamic-update-slice_fusion.1, bf16[3072,1024]{1,0:T(8,128)(2,1)} %all-gather.9.cloned.1.call-done), kind=kLoop, calls=%fused_computation.44 | loop fusion | bytes 12582912 | tf_op jit(solution)/shard_map/dynamic_update_slice | solution.py:43
  212.8 0.0 copy-done.7
  212.8 0.0 copy-done.3
  212.8 10.0 %fusion.7 = f32[256,3072]{1,0:T(8,128)S(1)} fusion(bf16[3072,3072]{1,0:T(8,128)(2,1)} %constant_dynamic-update-slice_fusion, bf16[256,3072]{1,0:T(8,128)(2,1)S(1)} %copy-done.3, f32[3072]{0:T(1024)S(1)} %copy-done.7, f32[256]{0:T(256)S(1)} %add_rsqrt_fusion.2, f32[256]{0:T(256)S(1)} %broadcast_multiply_fusion.2), kind=kOutput, calls=%fused_computation.13 | convolution fusion | flops 4835770368 | bytes 23607296 | tf_op jit(solution)/shard_map/dot_general | solution.py:62
  222.7 0.0 copy-start
  222.7 1.0 slice.25
  223.7 2.3 copy.14
  226.0 0.2 slice_bitcast_fusion.1
  226.3 0.0 copy-done
  226.3 0.2 copy.17
  226.5 0.2 copy.20
  226.7 0.3 reduce_sum.65
  227.0 0.3 reduce_sum.67
  227.4 0.6 multiply_reduce_fusion.2
  228.1 0.0 copy-start.1
  228.1 0.0 copy-start.5
  228.1 0.0 copy-start.6
  228.1 0.6 multiply_reduce_fusion.1
  228.8 0.3 mul.78
  229.1 0.3 sub.45
  229.5 0.3 mul.84
  229.8 0.3 sub.49
  230.1 0.0 copy-done.1
  230.2 0.0 copy-done.5
  230.2 0.0 copy-done.6
  230.2 1.3 fusion.17
  231.5 0.0 copy-start.4
  231.5 2.1 fusion.37
  233.6 0.0 copy-done.4
  233.6 1.9 convolution_convert_fusion.1
  235.5 35.8 %all-gather.11.cloned.1.call-done = bf16[3072,1024]{1,0:T(8,128)(2,1)} async-done(((bf16[384,1024]{1,0:T(8,128)(2,1)}), bf16[3072,1024]{1,0:T(8,128)(2,1)}) %all-gather.11.cloned.1.call-update) | async-done | bytes 6291472 | tf_op jit(solution)/shard_map/all_gather | solution.py:74
  271.3 5.8 %convolution_convert_fusion = bf16[256,3072]{1,0:T(8,128)(2,1)} fusion(bf16[256,1024]{0,1:T(8,128)(2,1)S(1)} %bitcast.83, bf16[3072,1024]{1,0:T(8,128)(2,1)} %all-gather.11.cloned.1.call-done), kind=kOutput, calls=%fused_computation.3 | convolution fusion | flops 1611399168 | bytes 8388608 | tf_op jit(solution)/shard_map/dot_general | solution.py:76
  277.1 0.0 reduce-scatter.2.cloned.1.call-update
  277.1 29.9 %reduce-scatter.2.cloned.1.call-done = bf16[64,3072]{1,0:T(8,128)(2,1)} async-done(((bf16[256,3072]{1,0:T(8,128)(2,1)}), bf16[64,3072]{1,0:T(8,128)(2,1)}) %reduce-scatter.2.cloned.1.call-update) | async-done | bytes 393232 | tf_op jit(solution)/shard_map/reduce_scatter | solution.py:75
  (6 shorter events, 0.1 us)
Async XLA Ops:
  6.5 2.8 copy-start.2
  6.5 69.9 %all-gather.5.cloned.1.call-start = ((), (), s32[]{:S(2)}) async-start(), calls=%async_computation.1 | async-start | bytes 7077888 | tf_op jit(solution)/shard_map/all_gather | solution.py:55
  7.3 134.2 %all-gather.7.cloned.1.call-start = ((), (), s32[]{:S(2)}) async-start(), calls=%async_computation.2 | async-start | bytes 7077888 | tf_op jit(solution)/shard_map/all_gather | solution.py:56
  8.0 198.5 %all-gather.9.cloned.1.call-start = ((), (), s32[]{:S(2)}) async-start(), calls=%async_computation.3 | async-start | bytes 7077888 | tf_op jit(solution)/shard_map/all_gather | solution.py:57
  8.7 262.6 %all-gather.11.cloned.1.call-start = ((), (), s32[]{:S(2)}) async-start(), calls=%async_computation.4 | async-start | bytes 7077888 | tf_op jit(solution)/shard_map/all_gather | solution.py:74
  9.3 297.8 %reduce-scatter.2.cloned.1.call-start = ((), (), s32[]{:S(2)}) async-start(), calls=%async_computation.5 | async-start | bytes 1966080 | tf_op jit(solution)/shard_map/reduce_scatter | solution.py:75
  147.8 65.0 %copy-start.7 = (f32[3072]{0:T(1024)S(1)}, f32[3072]{0:T(1024)}, u32[]{:S(2)}) copy-start(f32[3072]{0:T(1024)} %param.9) | copy-start | bytes 36868
  206.5 6.3 %copy-start.3 = (bf16[256,3072]{1,0:T(8,128)(2,1)S(1)}, bf16[256,3072]{1,0:T(8,128)(2,1)}, u32[]{:S(2)}) copy-start(bf16[256,3072]{1,0:T(8,128)(2,1)} %param.8) | copy-start | bytes 4718596
  222.7 3.5 %copy-start = (f32[256,3072]{1,0:T(8,128)}, f32[256,3072]{1,0:T(8,128)S(1)}, u32[]{:S(2)}) copy-start(f32[256,3072]{1,0:T(8,128)S(1)} %fusion.7) | copy-start | bytes 9437188
  228.1 2.1 copy-start.1
  228.1 2.1 copy-start.5
  228.1 2.1 copy-start.6
  231.5 2.2 copy-start.4
Sparse Core Ops, SparseCore 0:
  9.0 67.4 all-gather.4
  78.1 63.3 all-gather.6
  143.1 63.3 all-gather.8
  208.0 63.3 all-gather.10
  277.3 29.7 reduce-scatter.1
where the time goes:
time: 314 us
  waiting for transfers between devices  249 us (79%)
  local copies, waits for them, and re-layouts  27.6 us (9%)
  matrix products  19.8 us (6%)
  between operations  13.3 us (4%)
  other arithmetic  4.16 us (1%)
    all_gather x1, waiting for transfers between devices, on_device(): lax.all_gather(q_weight, 'dp', axis=0, tiled=True)  66.2 us
    all_gather x1, waiting for transfers between devices, on_device(): lax.all_gather(v_weight, 'dp', axis=0, tiled=True)  58.7 us
    all_gather x1, waiting for transfers between devices, on_device(): lax.all_gather(k_weight, 'dp', axis=0, tiled=True)  55.3 us
    all_gather x1, waiting for transfers between devices, on_device(): out_full = lax.all_gather(out_weight, 'dp', axis=0, tiled=True)  35.8 us
    reduce_scatter x1, waiting for transfers between devices, on_device(): lax.psum_scatter(lax.dot_general(context, out_full, (((1,), (1,)), ((), (...  29.9 us
    dot_general x1, matrix products, on_device(): combined = jnp.dot(normed, projections, preferred_element_type=jnp.float32)  9.96 us
    dynamic_update_slice x1, local copies, waits for them, and re-layouts, place_three(): holder = lax.dynamic_update_slice(holder, pieces[0], (offset, 0))  9.71 us
    dynamic_update_slice x1, local copies, waits for them, and re-layouts, place_three(): holder = lax.dynamic_update_slice(holder, pieces[1], (offset, local_width))  6.32 us
  transfers between devices with their start and end apart: 5, of which 5 were waited for; matrix products, arithmetic and copies ran while one was open for 15% of the time, Pallas kernels for 0%

commit v1 on v0

--- a/solution.py
+++ b/solution.py
@@ -1,8 +1,11 @@
+import functools
 import math
 
 import jax
 import jax.numpy as jnp
 from jax import lax
+from jax.experimental import pallas as pl
+from jax.experimental.pallas import tpu as pltpu
 from jax.sharding import PartitionSpec as P
 
 HEAD_DIM = 128
@@ -43,7 +46,7 @@
     return lax.dynamic_update_slice(holder, pieces[2], (offset, 2 * local_width))
 
 
-def on_device(tokens, ln_gain, q_weight, k_weight, v_weight, q_gain, k_gain, out_weight):
+def gathered_weights(tokens, ln_gain, q_weight, k_weight, v_weight, q_gain, k_gain, out_weight):
     normed = layer_norm(tokens.astype(jnp.float32), ln_gain).astype(jnp.bfloat16)
     token_count = normed.shape[0]
     local_width = q_weight.shape[1]
@@ -82,6 +85,460 @@
     )
 
 
+MESH = pl.DeviceIdType.MESH
+
+
+def exchange_kernel(
+    pairs, groups, tokens, ln_gain, q_w, k_w, v_w, q_gain, k_gain, out_w, result,
+    raw, normed, weights, out_rows, projected, context, partial, arrived, summed, final,
+    local_sem, up_send, down_send, token_recv, peer_send, peer_recv,
+    w_send, w_recv, own_send, own_recv, pass_send, pass_recv, out_send, out_recv,
+    c_up, c_down, c_recv, p_send, p_recv, f_send, f_recv,
+):
+    dp = lax.axis_index("dp")
+    group = lax.axis_index("mp")
+    pair = dp // 2
+    core = dp % 2
+    rows = tokens.shape[0]
+    part = rows // groups
+    shard = q_w.shape[0]
+    width = q_w.shape[1] // pairs
+    span = 2 * shard
+
+    def at_pair(other):
+        return (other * 2 + core, group)
+
+    partner = (pair * 2 + (1 - core), group)
+
+    def at_group(other):
+        return (dp, other)
+
+    def remote(source, target, send, recv, device):
+        return pltpu.make_async_remote_copy(
+            src_ref=source, dst_ref=target, send_sem=send, recv_sem=recv,
+            device_id=device, device_id_type=MESH,
+        )
+
+    greeted = pltpu.get_barrier_semaphore()
+    for step in range(1, pairs):
+        pl.semaphore_signal(
+            greeted, inc=1, device_id=at_pair((pair + step) % pairs), device_id_type=MESH
+        )
+    for step in range(1, groups):
+        pl.semaphore_signal(
+            greeted, inc=1, device_id=at_group((group + step) % groups), device_id_type=MESH
+        )
+    pl.semaphore_signal(greeted, inc=1, device_id=partner, device_id_type=MESH)
+
+    projections = (q_w, k_w, v_w)
+    own_columns = pl.ds(pl.multiple_of(pair * width, width), width)
+    quarter = pl.ds(pl.multiple_of(group * part, part), part)
+    locals_ = [pltpu.make_async_copy(tokens, raw.at[pair], local_sem.at[0])]
+    for t in range(3):
+        locals_.append(
+            pltpu.make_async_copy(
+                projections[t].at[:, own_columns],
+                weights.at[pair, core, :, pl.ds(t * width, width)],
+                local_sem.at[1 + t],
+            )
+        )
+    locals_.append(pltpu.make_async_copy(out_w, out_rows.at[core], local_sem.at[4]))
+    for copy in locals_:
+        copy.start()
+    pl.semaphore_wait(greeted, pairs + groups - 1)
+
+    def first_hop(up):
+        return remote(
+            tokens.at[quarter, :], raw.at[pair, quarter, :],
+            (up_send if up else down_send).at[pair], token_recv.at[pair],
+            at_pair(pair + 1 if up else pair - 1),
+        )
+
+    def next_hop(block, up):
+        return remote(
+            raw.at[block, quarter, :], raw.at[block, quarter, :],
+            (up_send if up else down_send).at[block], token_recv.at[block],
+            at_pair(pair + 1 if up else pair - 1),
+        )
+
+    def to_peer(block, step):
+        return remote(
+            raw.at[block, quarter, :], raw.at[block, quarter, :],
+            peer_send.at[block, step - 1], peer_recv.at[block, group],
+            at_group((group + step) % groups),
+        )
+
+    def from_peer(block, step):
+        other = (group + step) % groups
+        there = raw.at[block, pl.ds(pl.multiple_of(other * part, part), part), :]
+        return remote(
+            there, there, peer_send.at[block, step - 1], peer_recv.at[block, other],
+            at_group(other),
+        )
+
+    def weight_to(other, t):
+        return remote(
+            projections[t].at[:, pl.ds(pl.multiple_of(other * width, width), width)],
+            weights.at[pair, core, :, pl.ds(t * width, width)],
+            w_send.at[other, t], w_recv.at[pair, t], at_pair(other),
+        )
+
+    def weight_from(other, t):
+        there = weights.at[other, core, :, pl.ds(t * width, width)]
+        return remote(there, there, w_send.at[other, t], w_recv.at[other, t], at_pair(other))
+
+    def own_weight(t):
+        return remote(
+            projections[t].at[:, own_columns],
+            weights.at[pair, core, :, pl.ds(t * width, width)],
+            own_send.at[t], own_recv.at[t], partner,
+        )
+
+    def partner_weight(t):
+        there = weights.at[pair, 1 - core, :, pl.ds(t * width, width)]
+        return remote(there, there, own_send.at[t], own_recv.at[t], partner)
+
+    def pass_on(other):
+        return remote(
+            weights.at[other, core], weights.at[other, core],
+            pass_send.at[other], pass_recv.at[other], partner,
+        )
+
+    def passed(other):
+        there = weights.at[other, 1 - core]
+        return remote(there, there, pass_send.at[other], pass_recv.at[other], partner)
+
+    def out_over():
+        return remote(out_w, out_rows.at[core], out_send, out_recv, partner)
+
+    def out_back():
+        there = out_rows.at[1 - core]
+        return remote(there, there, out_send, out_recv, partner)
+
+    has_up = pair + 1 < pairs
+    has_down = pair > 0
+
+    @pl.when(has_up)
+    def _():
+        first_hop(True).start()
+
+    @pl.when(has_down)
+    def _():
+        first_hop(False).start()
+
+    def send_weights(t):
+        for distance in range(pairs - 1, 0, -1):
+            @pl.when(pair + distance < pairs)
+            def _():
+                weight_to(pair + distance, t).start()
+
+            @pl.when(pair - distance >= 0)
+            def _():
+                weight_to(pair - distance, t).start()
+
+    send_weights(0)
+    for t in range(3):
+        own_weight(t).start()
+    out_over().start()
+
+    def normalise(block):
+        @pl.loop(0, rows // 16)
+        def _(chunk):
+            place = pl.ds(pl.multiple_of(chunk * 16, 16), 16)
+            values = raw[block, place, :].astype(jnp.float32)
+            average = jnp.mean(values, axis=-1, keepdims=True)
+            centred = values - average
+            variance = jnp.mean(centred * centred, axis=-1, keepdims=True)
+            scaled = centred * lax.rsqrt(variance + epsilon) * ln_gain[...]
+            scaled = scaled.astype(jnp.bfloat16)
+            for p in range(pairs):
+                normed[p, block, place, :] = scaled[:, p * span : (p + 1) * span]
+
+    for copy in locals_:
+        copy.wait()
+    normalise(pair)
+
+    def relay(block, up):
+        next_hop(block, up).wait_recv()
+
+        @pl.when(has_up if up else has_down)
+        def _():
+            next_hop(block, up).start()
+
+        for step in range(1, groups):
+            to_peer(block, step).start()
+
+    for distance in range(1, pairs):
+        @pl.when(pair - distance >= 0)
+        def _():
+            relay(pair - distance, True)
+
+        @pl.when(pair + distance < pairs)
+        def _():
+            relay(pair + distance, False)
+
+        if distance < 3:
+            send_weights(distance)
+    for t in range(pairs, 3):
+        send_weights(t)
+
+    def project(block, first):
+        @pl.loop(0, pairs)
+        def _(image):
+            product = jnp.dot(
+                normed[block, image], weights[block].reshape(span, 3 * width),
+                preferred_element_type=jnp.float32,
+            )
+            projected[image] = product if first else projected[image] + product
+
+    @pl.loop(1, pairs)
+    def _(k):
+        block = (pair + k) % pairs
+        for step in range(1, groups):
+            from_peer(block, step).wait_recv()
+        normalise(block)
+
+    for t in range(3):
+        partner_weight(t).wait_recv()
+    project(pair, True)
+
+    @pl.loop(1, pairs)
+    def _(k):
+        block = (pair + k) % pairs
+        for t in range(3):
+            weight_from(block, t).wait_recv()
+        pass_on(block).start()
+
+    @pl.loop(1, pairs)
+    def _(k):
+        block = (pair + k) % pairs
+        passed(block).wait_recv()
+        project(block, False)
+
+    def head_layer_norm(values, scale_gain):
+        average = jnp.mean(values, axis=-1, keepdims=True)
+        centred = values - average
+        variance = jnp.mean(centred * centred, axis=-1, keepdims=True)
+        return (centred * lax.rsqrt(variance + epsilon) * scale_gain).astype(jnp.bfloat16)
+
+    def context_hop(block, image, up):
+        return remote(
+            context.at[block, image], context.at[block, image],
+            (c_up if up else c_down).at[block, image], c_recv.at[block, image],
+            at_pair(pair + 1 if up else pair - 1),
+        )
+
+    @pl.loop(0, pairs)
+    def _(image):
+        for h in range(width // HEAD_DIM):
+            lanes = slice(h * HEAD_DIM, (h + 1) * HEAD_DIM)
+            queries = head_layer_norm(projected[image, :, lanes], q_gain[pair, :, lanes])
+            shifted = slice(width + h * HEAD_DIM, width + (h + 1) * HEAD_DIM)
+            key_rows = head_layer_norm(projected[image, :, shifted], k_gain[pair, :, lanes])
+            last = slice(2 * width + h * HEAD_DIM, 2 * width + (h + 1) * HEAD_DIM)
+            value_rows = projected[image, :, last].astype(jnp.bfloat16)
+            scores = lax.dot_general(
+                queries, key_rows, (((1,), (1,)), ((), ())), preferred_element_type=jnp.float32
+            ) * (1.0 / math.sqrt(HEAD_DIM))
+            highest = jnp.max(scores, axis=-1, keepdims=True)
+            spread = jnp.exp(scores - highest)
+            probs = (spread / jnp.sum(spread, axis=-1, keepdims=True)).astype(jnp.bfloat16)
+            mixed = jnp.dot(probs, value_rows, preferred_element_type=jnp.float32)
+            context[pair, image, :, lanes] = mixed.astype(jnp.bfloat16)
+
+        @pl.when(has_up)
+        def _():
+            context_hop(pair, image, True).start()
+
+        @pl.when(has_down)
+        def _():
+            context_hop(pair, image, False).start()
+
+    def pass_context(block, image, up):
+        context_hop(block, image, up).wait_recv()
+
+        @pl.when(has_up if up else has_down)
+        def _():
+            context_hop(block, image, up).start()
+
+    def partial_to(image, step):
+        other = (group + step) % groups
+        return remote(
+            partial.at[image, pl.ds(pl.multiple_of(other * part, part), part), :],
+            arrived.at[image, group],
+            p_send.at[image, step - 1], p_recv.at[image, group], at_group(other),
+        )
+
+    def partial_from(image, step):
+        other = (group + step) % groups
+        there = arrived.at[image, other]
+        return remote(there, there, p_send.at[image, step - 1], p_recv.at[image, other], at_group(other))
+
+    out_back().wait_recv()
+
+    @pl.loop(0, pairs)
+    def _(image):
+        for distance in range(1, pairs):
+            @pl.when(pair - distance >= 0)
+            def _():
+                pass_context(pair - distance, image, True)
+
+            @pl.when(pair + distance < pairs)
+            def _():
+                pass_context(pair + distance, image, False)
+
+        for c in range(2):
+            total = None
+            for p in range(pairs):
+                product = lax.dot_general(
+                    context[p, image], out_rows[c, :, p * width : (p + 1) * width],
+                    (((1,), (1,)), ((), ())), preferred_element_type=jnp.float32,
+                )
+                total = product if total is None else total + product
+            partial[image, :, c * shard : (c + 1) * shard] = total.astype(jnp.bfloat16)
+        for step in range(1, groups):
+            partial_to(image, step).start()
+
+    def final_to(image):
+        return remote(
+            summed.at[image], final.at[pair], f_send.at[image], f_recv.at[pair], at_pair(image)
+        )
+
+    def final_from(other):
+        return remote(
+            final.at[other], final.at[other], f_send.at[other], f_recv.at[other], at_pair(other)
+        )
+
+    @pl.loop(0, pairs)
+    def _(image):
+        total = partial[image, quarter, :].astype(jnp.float32)
+        for step in range(1, groups):
+            partial_from(image, step).wait_recv()
+            total = total + arrived[image, (group + step) % groups].astype(jnp.float32)
+        summed[image] = total.astype(jnp.bfloat16)
+
+        @pl.when(image != pair)
+        def _():
+            final_to(image).start()
+
+        @pl.when(image == pair)
+        def _():
+            final[pair] = summed[image]
+
+    @pl.loop(1, pairs)
+    def _(k):
+        final_from((pair + k) % pairs).wait_recv()
+
+    for p in range(pairs):
+        result[:, p * span : (p + 1) * span] = final[p]
+
+    @pl.when(has_up)
+    def _():
+        first_hop(True).wait_send()
+
+    @pl.when(has_down)
+    def _():
+        first_hop(False).wait_send()
+
+    for t in range(3):
+        own_weight(t).wait_send()
+    out_over().wait_send()
+    for distance in range(1, pairs):
+        for up in (True, False):
+            inside = pair - distance >= 0 if up else pair + distance < pairs
+            block = pair - distance if up else pair + distance
+
+            @pl.when(inside & (has_up if up else has_down))
+            def _():
+                next_hop(block, up).wait_send()
+
+                @pl.loop(0, pairs)
+                def _(image):
+                    context_hop(block, image, up).wait_send()
+
+    @pl.loop(0, pairs)
+    def _(image):
+        @pl.when(has_up)
+        def _():
+            context_hop(pair, image, True).wait_send()
+
+        @pl.when(has_down)
+        def _():
+            context_hop(pair, image, False).wait_send()
+
+        for step in range(1, groups):
+            partial_to(image, step).wait_send()
+
+    @pl.loop(1, pairs)
+    def _(k):
+        block = (pair + k) % pairs
+        for t in range(3):
+            weight_to(block, t).wait_send()
+        pass_on(block).wait_send()
+        for step in range(1, groups):
+            to_peer(block, step).wait_send()
+        final_to(block).wait_send()
+
+
+def exchanged_heads(pairs, groups, tokens, ln_gain, q_w, k_w, v_w, q_gain, k_gain, out_w):
+    rows, features = tokens.shape
+    shard, local_width = q_w.shape
+    width = local_width // pairs
+    part = rows // groups
+    dma = pltpu.SemaphoreType.DMA
+    in_hbm = pl.BlockSpec(memory_space=pl.ANY)
+    in_vmem = pl.BlockSpec(memory_space=pltpu.VMEM)
+    bf16 = jnp.bfloat16
+    return pl.pallas_call(
+        functools.partial(exchange_kernel, pairs, groups),
+        out_shape=jax.ShapeDtypeStruct((part, features), bf16),
+        in_specs=[in_hbm, in_vmem, in_hbm, in_hbm, in_hbm, in_vmem, in_vmem, in_hbm],
+        out_specs=in_vmem,
+        scratch_shapes=[
+            pltpu.VMEM((pairs, rows, features), bf16),
+            pltpu.VMEM((pairs, pairs, rows, 2 * shard), bf16),
+            pltpu.VMEM((pairs, 2, shard, 3 * width), bf16),
+            pltpu.VMEM((2, shard, local_width), bf16),
+            pltpu.VMEM((pairs, rows, 3 * width), jnp.float32),
+            pltpu.VMEM((pairs, pairs, rows, width), bf16),
+            pltpu.VMEM((pairs, rows, 2 * shard), bf16),
+            pltpu.VMEM((pairs, groups, part, 2 * shard), bf16),
+            pltpu.VMEM((pairs, part, 2 * shard), bf16),
+            pltpu.VMEM((pairs, part, 2 * shard), bf16),
+            dma((5,)), dma((pairs,)), dma((pairs,)), dma((pairs,)),
+            dma((pairs, groups)), dma((pairs, groups)),
+            dma((pairs, 3)), dma((pairs, 3)), dma((3,)), dma((3,)),
+            dma((pairs,)), dma((pairs,)), dma, dma,
+            dma((pairs, pairs)), dma((pairs, pairs)), dma((pairs, pairs)),
+            dma((pairs, groups)), dma((pairs, groups)), dma((pairs,)), dma((pairs,)),
+        ],
+        compiler_params=pltpu.CompilerParams(
+            collective_id=0, has_side_effects=True, vmem_limit_bytes=60 * 1024 * 1024
+        ),
+    )(
+        tokens, ln_gain.reshape(1, features), q_w, k_w, v_w,
+        q_gain.reshape(pairs, 1, width), k_gain.reshape(pairs, 1, width), out_w,
+    )
+
+
+def on_device(tokens, ln_gain, q_w, k_w, v_w, q_gain, k_gain, out_w):
+    devices = lax.axis_size("dp")
+    groups = lax.axis_size("mp")
+    pairs = devices // 2
+    fits = (
+        devices % 2 == 0
+        and pairs > 1
+        and q_w.shape[1] % (pairs * HEAD_DIM) == 0
+        and q_w.shape[0] % 128 == 0
+        and tokens.shape[0] == IMG_TOKENS
+        and tokens.shape[0] % (16 * groups) == 0
+        and pairs <= 4
+    )
+    if fits:
+        return exchanged_heads(pairs, groups, tokens, ln_gain, q_w, k_w, v_w, q_gain, k_gain, out_w)
+    return gathered_weights(tokens, ln_gain, q_w, k_w, v_w, q_gain, k_gain, out_w)
+
+
 def solution(mesh):
     in_specs = (
         P("dp", None),

time: 314 us -> 160 us (0.51)
  waiting for transfers between devices: 249 us -> 0 us
  Pallas kernels: 0 us -> 156 us
  local copies, waits for them, and re-layouts: 27.6 us -> 1.77 us
  matrix products: 19.8 us -> 0 us
  between operations: 13.3 us -> 0.01 us
  other arithmetic: 4.16 us -> 0 us
    all_gather x4 -> x0, waiting for transfers between devices: 216 us -> none  [the longest x1 66.2 us: on_device(): lax.all_gather(q_weight, 'dp', axis=0, tiled=True)]
    pallas_call x0 -> x1, Pallas kernels: none -> 156 us  [exchanged_heads(): pl.pallas_call(functools.partial(exchange_kernel, pairs, groups), out_sha...]
    reduce_scatter x1 -> x0, waiting for transfers between devices: 29.9 us -> none  [on_device(): lax.psum_scatter(lax.dot_general(context, out_full, (((1,), (1,)), ((), (...]
    dynamic_update_slice x3 -> x0, local copies, waits for them, and re-layouts: 22.3 us -> none  [the longest x1 9.71 us: place_three(): holder = lax.dynamic_update_slice(holder, pieces[0], (offset, 0))]
    dot_general x3 -> x0, matrix products: 17.7 us -> none  [the longest x1 9.96 us: on_device(): combined = jnp.dot(normed, projections, preferred_element_type=jnp.float32)]
  transfers between devices with their start and end apart: 5 -> 0, of which waited for: 5 -> 0; matrix products, arithmetic and copies ran while one was open for 15% -> 0% of each run, Pallas kernels for 0% -> 0%
where the time goes in v1:
time: 160 us; the launch traced here: 158 us
  Pallas kernels  156 us (98%)
  local copies, waits for them, and re-layouts  1.77 us (1%)
    pallas_call x1, Pallas kernels, exchanged_heads(): pl.pallas_call(functools.partial(exchange_kernel, pairs, groups), out_sha...  156 us

profile of v1, /device:TPU:0, one launch (start us, length us, event | category | flops | bytes accessed | tf_op | source)
XLA Modules:
  0.0 157.9 jit_solution(16080387186136082987)
XLA Ops:
  0.0 156.1 %shard_map.82 = bf16[64,3072]{1,0:T(8,128)(2,1)} custom-call(bf16[256,3072]{1,0:T(8,128)(2,1)} %tokens.1, f32[1,3072]{1,0:T(1,128)} %bitcast.3, bf16[384,1024]{1,0:T(8,128)(2,1)} %q_w.1, bf16[384,1024]{1,0:T(8,128)(2,1)} %k_w.1, bf16[384,1024]{1,0:T(8,128)(2,1)} %v_w.1, f32[4,1,256]{2,1,0:T(1,128)} %bitcast.4, f32[4,1,256]{2,1,0:T(1,128)} %bitcast.5, ...), custom_call_target="tpu_custom_call" | custom-call | tf_op jit(solution)/shard_map/pallas_call | solution.py:492
  156.1 1.8 %copy.10 = bf16[64,3072]{1,0:T(8,128)(2,1)} copy(bf16[64,3072]{1,0:T(8,128)(2,1)} %shard_map.82) | data formatting | bytes 786432

commit v2 on v1

--- a/solution.py
+++ b/solution.py
@@ -90,7 +90,7 @@
 
 def exchange_kernel(
     pairs, groups, tokens, ln_gain, q_w, k_w, v_w, q_gain, k_gain, out_w, result,
-    raw, normed, weights, out_rows, projected, context, partial, arrived, summed, final,
+    raw, normed, weights, out_rows, context, partial, arrived, summed, final,
     local_sem, up_send, down_send, token_recv, peer_send, peer_recv,
     w_send, w_recv, own_send, own_recv, pass_send, pass_recv, out_send, out_recv,
     c_up, c_down, c_recv, p_send, p_recv, f_send, f_recv,
@@ -104,6 +104,7 @@
     shard = q_w.shape[0]
     width = q_w.shape[1] // pairs
     span = 2 * shard
+    heads = width // HEAD_DIM
 
     def at_pair(other):
         return (other * 2 + core, group)
@@ -131,18 +132,24 @@
     pl.semaphore_signal(greeted, inc=1, device_id=partner, device_id_type=MESH)
 
     projections = (q_w, k_w, v_w)
-    own_columns = pl.ds(pl.multiple_of(pair * width, width), width)
+
+    def columns(other, h, t):
+        start = pl.multiple_of(other * width + h * HEAD_DIM, HEAD_DIM)
+        return projections[t].at[:, pl.ds(start, HEAD_DIM)]
+
+    def slot(h, block, side, t):
+        return weights.at[h, block, side, :, pl.ds(t * HEAD_DIM, HEAD_DIM)]
+
     quarter = pl.ds(pl.multiple_of(group * part, part), part)
     locals_ = [pltpu.make_async_copy(tokens, raw.at[pair], local_sem.at[0])]
-    for t in range(3):
-        locals_.append(
-            pltpu.make_async_copy(
-                projections[t].at[:, own_columns],
-                weights.at[pair, core, :, pl.ds(t * width, width)],
-                local_sem.at[1 + t],
+    locals_.append(pltpu.make_async_copy(out_w, out_rows.at[core], local_sem.at[1]))
+    for h in range(heads):
+        for t in range(3):
+            locals_.append(
+                pltpu.make_async_copy(
+                    columns(pair, h, t), slot(h, pair, core, t), local_sem.at[2 + 3 * h + t]
+                )
             )
-        )
-    locals_.append(pltpu.make_async_copy(out_w, out_rows.at[core], local_sem.at[4]))
     for copy in locals_:
         copy.start()
     pl.semaphore_wait(greeted, pairs + groups - 1)
@@ -161,52 +168,59 @@
             at_pair(pair + 1 if up else pair - 1),
         )
 
-    def to_peer(block, step):
-        return remote(
-            raw.at[block, quarter, :], raw.at[block, quarter, :],
-            peer_send.at[block, step - 1], peer_recv.at[block, group],
-            at_group((group + step) % groups),
-        )
-
-    def from_peer(block, step):
-        other = (group + step) % groups
-        there = raw.at[block, pl.ds(pl.multiple_of(other * part, part), part), :]
-        return remote(
-            there, there, peer_send.at[block, step - 1], peer_recv.at[block, other],
-            at_group(other),
-        )
-
-    def weight_to(other, t):
-        return remote(
-            projections[t].at[:, pl.ds(pl.multiple_of(other * width, width), width)],
-            weights.at[pair, core, :, pl.ds(t * width, width)],
-            w_send.at[other, t], w_recv.at[pair, t], at_pair(other),
-        )
-
-    def weight_from(other, t):
-        there = weights.at[other, core, :, pl.ds(t * width, width)]
-        return remote(there, there, w_send.at[other, t], w_recv.at[other, t], at_pair(other))
-
-    def own_weight(t):
-        return remote(
-            projections[t].at[:, own_columns],
-            weights.at[pair, core, :, pl.ds(t * width, width)],
-            own_send.at[t], own_recv.at[t], partner,
-        )
-
-    def partner_weight(t):
-        there = weights.at[pair, 1 - core, :, pl.ds(t * width, width)]
-        return remote(there, there, own_send.at[t], own_recv.at[t], partner)
-
-    def pass_on(other):
-        return remote(
-            weights.at[other, core], weights.at[other, core],
-            pass_send.at[other], pass_recv.at[other], partner,
-        )
-
-    def passed(other):
-        there = weights.at[other, 1 - core]
-        return remote(there, there, pass_send.at[other], pass_recv.at[other], partner)
+    beside = group + 1 - 2 * (group % 2)
+    across = (group + 2) % 4
+    first = jnp.where(core == 0, beside, across)
+    second = jnp.where(core == 0, across, beside)
+    opposite = 3 - group
+
+    def part_of(block, other):
+        return raw.at[block, pl.ds(pl.multiple_of(other * part, part), part), :]
+
+    def peer_copy(block, owner, place, other):
+        there = part_of(block, owner)
+        return remote(
+            there, there, peer_send.at[block, place], peer_recv.at[block, owner], at_group(other)
+        )
+
+    def to_first(block):
+        return peer_copy(block, group, 0, first)
+
+    def to_second(block):
+        return peer_copy(block, group, 1, second)
+
+    def cross(block):
+        return peer_copy(block, first, 2, second)
+
+    def from_peer(block, owner):
+        return peer_copy(block, owner, 0, first)
+
+    def weight_to(other, h, t):
+        return remote(
+            columns(other, h, t), slot(h, pair, core, t),
+            w_send.at[other, h, t], w_recv.at[pair, h, t], at_pair(other),
+        )
+
+    def weight_from(other, h, t):
+        there = slot(h, other, core, t)
+        return remote(there, there, w_send.at[other, h, t], w_recv.at[other, h, t], at_pair(other))
+
+    def own_weight(h, t):
+        return remote(
+            columns(pair, h, t), slot(h, pair, core, t), own_send.at[h, t], own_recv.at[h, t], partner
+        )
+
+    def partner_weight(h, t):
+        there = slot(h, pair, 1 - core, t)
+        return remote(there, there, own_send.at[h, t], own_recv.at[h, t], partner)
+
+    def pass_on(other, h):
+        there = weights.at[h, other, core]
+        return remote(there, there, pass_send.at[other, h], pass_recv.at[other, h], partner)
+
+    def passed(other, h):
+        there = weights.at[h, other, 1 - core]
+        return remote(there, there, pass_send.at[other, h], pass_recv.at[other, h], partner)
 
     def out_over():
         return remote(out_w, out_rows.at[core], out_send, out_recv, partner)
@@ -226,19 +240,27 @@
     def _():
         first_hop(False).start()
 
-    def send_weights(t):
-        for distance in range(pairs - 1, 0, -1):
-            @pl.when(pair + distance < pairs)
-            def _():
-                weight_to(pair + distance, t).start()
-
-            @pl.when(pair - distance >= 0)
-            def _():
-                weight_to(pair - distance, t).start()
-
-    send_weights(0)
-    for t in range(3):
-        own_weight(t).start()
+    def send_weights(up, some):
+        for h in some:
+            for distance in range(pairs - 1, 0, -1) if h == 0 else range(1, pairs):
+                other = pair + distance if up else pair - distance
+
+                @pl.when(other < pairs if up else other >= 0)
+                def _():
+                    for t in range(3):
+                        weight_to(other, h, t).start()
+
+    @pl.when(pair == 0)
+    def _():
+        send_weights(True, range(1))
+
+    @pl.when(pair == pairs - 1)
+    def _():
+        send_weights(False, range(1))
+
+    for h in range(heads):
+        for t in range(3):
+            own_weight(h, t).start()
     out_over().start()
 
     def normalise(block):
@@ -265,8 +287,8 @@
         def _():
             next_hop(block, up).start()
 
-        for step in range(1, groups):
-            to_peer(block, step).start()
+        to_first(block).start()
+        to_second(block).start()
 
     for distance in range(1, pairs):
         @pl.when(pair - distance >= 0)
@@ -277,43 +299,54 @@
         def _():
             relay(pair + distance, False)
 
-        if distance < 3:
-            send_weights(distance)
-    for t in range(pairs, 3):
-        send_weights(t)
-
-    def project(block, first):
-        @pl.loop(0, pairs)
-        def _(image):
-            product = jnp.dot(
-                normed[block, image], weights[block].reshape(span, 3 * width),
-                preferred_element_type=jnp.float32,
-            )
-            projected[image] = product if first else projected[image] + product
-
-    @pl.loop(1, pairs)
-    def _(k):
-        block = (pair + k) % pairs
-        for step in range(1, groups):
-            from_peer(block, step).wait_recv()
+        @pl.when(has_up & (pair == distance))
+        def _():
+            send_weights(True, range(1))
+
+        @pl.when(has_down & (pair == pairs - 1 - distance))
+        def _():
+            send_weights(False, range(1))
+
+    def cross_tokens(block):
+        from_peer(block, first).wait_recv()
+        cross(block).start()
+
+    for distance in range(1, pairs):
+        @pl.when(pair - distance >= 0)
+        def _():
+            cross_tokens(pair - distance)
+
+        @pl.when(pair + distance < pairs)
+        def _():
+            cross_tokens(pair + distance)
+
+    send_weights(True, range(1, heads))
+    send_weights(False, range(1, heads))
+
+    def take_tokens(block):
+        from_peer(block, second).wait_recv()
+        from_peer(block, opposite).wait_recv()
         normalise(block)
 
-    for t in range(3):
-        partner_weight(t).wait_recv()
-    project(pair, True)
-
-    @pl.loop(1, pairs)
-    def _(k):
-        block = (pair + k) % pairs
-        for t in range(3):
-            weight_from(block, t).wait_recv()
-        pass_on(block).start()
-
-    @pl.loop(1, pairs)
-    def _(k):
-        block = (pair + k) % pairs
-        passed(block).wait_recv()
-        project(block, False)
+    def pass_weights(h):
+        @pl.loop(1, pairs)
+        def _(k):
+            block = (pair + k) % pairs
+            for t in range(3):
+                weight_from(block, h, t).wait_recv()
+            pass_on(block, h).start()
+
+    for distance in range(1, pairs):
+        if distance == pairs - 1:
+            pass_weights(0)
+
+        @pl.when(pair - distance >= 0)
+        def _():
+            take_tokens(pair - distance)
+
+        @pl.when(pair + distance < pairs)
+        def _():
+            take_tokens(pair + distance)
 
     def head_layer_norm(values, scale_gain):
         average = jnp.mean(values, axis=-1, keepdims=True)
@@ -321,22 +354,50 @@
         variance = jnp.mean(centred * centred, axis=-1, keepdims=True)
         return (centred * lax.rsqrt(variance + epsilon) * scale_gain).astype(jnp.bfloat16)
 
-    def context_hop(block, image, up):
-        return remote(
-            context.at[block, image], context.at[block, image],
-            (c_up if up else c_down).at[block, image], c_recv.at[block, image],
+    def context_hop(block, image, h, up):
+        there = context.at[block, image, :, pl.ds(h * HEAD_DIM, HEAD_DIM)]
+        return remote(
+            there, there,
+            (c_up if up else c_down).at[block, image, h], c_recv.at[block, image, h],
             at_pair(pair + 1 if up else pair - 1),
         )
 
-    @pl.loop(0, pairs)
-    def _(image):
-        for h in range(width // HEAD_DIM):
-            lanes = slice(h * HEAD_DIM, (h + 1) * HEAD_DIM)
-            queries = head_layer_norm(projected[image, :, lanes], q_gain[pair, :, lanes])
-            shifted = slice(width + h * HEAD_DIM, width + (h + 1) * HEAD_DIM)
-            key_rows = head_layer_norm(projected[image, :, shifted], k_gain[pair, :, lanes])
-            last = slice(2 * width + h * HEAD_DIM, 2 * width + (h + 1) * HEAD_DIM)
-            value_rows = projected[image, :, last].astype(jnp.bfloat16)
+    def pass_context(image, h, distance):
+        for up in (True, False):
+            block = pair - distance if up else pair + distance
+
+            @pl.when(block >= 0 if up else block < pairs)
+            def _():
+                context_hop(block, image, h, up).wait_recv()
+
+                @pl.when(has_up if up else has_down)
+                def _():
+                    context_hop(block, image, h, up).start()
+
+    for h in range(heads):
+        if h > 0:
+            pass_weights(h)
+        for t in range(3):
+            partner_weight(h, t).wait_recv()
+
+        @pl.loop(1, pairs)
+        def _(k):
+            passed((pair + k) % pairs, h).wait_recv()
+
+        lanes = slice(h * HEAD_DIM, (h + 1) * HEAD_DIM)
+
+        @pl.loop(0, pairs)
+        def _(image):
+            total = None
+            for p in range(pairs):
+                product = jnp.dot(
+                    normed[p, image], weights[h, p].reshape(span, 3 * HEAD_DIM),
+                    preferred_element_type=jnp.float32,
+                )
+                total = product if total is None else total + product
+            queries = head_layer_norm(total[:, :HEAD_DIM], q_gain[pair, :, lanes])
+            key_rows = head_layer_norm(total[:, HEAD_DIM : 2 * HEAD_DIM], k_gain[pair, :, lanes])
+            value_rows = total[:, 2 * HEAD_DIM :].astype(jnp.bfloat16)
             scores = lax.dot_general(
                 queries, key_rows, (((1,), (1,)), ((), ())), preferred_element_type=jnp.float32
             ) * (1.0 / math.sqrt(HEAD_DIM))
@@ -346,20 +407,24 @@
             mixed = jnp.dot(probs, value_rows, preferred_element_type=jnp.float32)
             context[pair, image, :, lanes] = mixed.astype(jnp.bfloat16)
 
-        @pl.when(has_up)
-        def _():
-            context_hop(pair, image, True).start()
-
-        @pl.when(has_down)
-        def _():
-            context_hop(pair, image, False).start()
-
-    def pass_context(block, image, up):
-        context_hop(block, image, up).wait_recv()
-
-        @pl.when(has_up if up else has_down)
-        def _():
-            context_hop(block, image, up).start()
+            @pl.when(has_up)
+            def _():
+                context_hop(pair, image, h, True).start()
+
+            @pl.when(has_down)
+            def _():
+                context_hop(pair, image, h, False).start()
+
+            if h > 0:
+                pass_context(image, h - 1, 1)
+
+    for distance in range(1, pairs):
+        @pl.loop(0, pairs)
+        def _(image):
+            for h in range(heads):
+                hop = distance + (1 if h < heads - 1 else 0)
+                if hop < pairs and not (distance == pairs - 1 and h == heads - 1):
+                    pass_context(image, h, hop)
 
     def partial_to(image, step):
         other = (group + step) % groups
@@ -378,14 +443,7 @@
 
     @pl.loop(0, pairs)
     def _(image):
-        for distance in range(1, pairs):
-            @pl.when(pair - distance >= 0)
-            def _():
-                pass_context(pair - distance, image, True)
-
-            @pl.when(pair + distance < pairs)
-            def _():
-                pass_context(pair + distance, image, False)
+        pass_context(image, heads - 1, pairs - 1)
 
         for c in range(2):
             total = None
@@ -440,8 +498,9 @@
     def _():
         first_hop(False).wait_send()
 
-    for t in range(3):
-        own_weight(t).wait_send()
+    for h in range(heads):
+        for t in range(3):
+            own_weight(h, t).wait_send()
     out_over().wait_send()
     for distance in range(1, pairs):
         for up in (True, False):
@@ -454,17 +513,20 @@
 
                 @pl.loop(0, pairs)
                 def _(image):
-                    context_hop(block, image, up).wait_send()
+                    for h in range(heads):
+                        context_hop(block, image, h, up).wait_send()
 
     @pl.loop(0, pairs)
     def _(image):
         @pl.when(has_up)
         def _():
-            context_hop(pair, image, True).wait_send()
+            for h in range(heads):
+                context_hop(pair, image, h, True).wait_send()
 
         @pl.when(has_down)
         def _():
-            context_hop(pair, image, False).wait_send()
+            for h in range(heads):
+                context_hop(pair, image, h, False).wait_send()
 
         for step in range(1, groups):
             partial_to(image, step).wait_send()
@@ -472,11 +534,13 @@
     @pl.loop(1, pairs)
     def _(k):
         block = (pair + k) % pairs
-        for t in range(3):
-            weight_to(block, t).wait_send()
-        pass_on(block).wait_send()
-        for step in range(1, groups):
-            to_peer(block, step).wait_send()
+        for h in range(heads):
+            for t in range(3):
+                weight_to(block, h, t).wait_send()
+            pass_on(block, h).wait_send()
+        to_first(block).wait_send()
+        to_second(block).wait_send()
+        cross(block).wait_send()
         final_to(block).wait_send()
 
 
@@ -484,6 +548,7 @@
     rows, features = tokens.shape
     shard, local_width = q_w.shape
     width = local_width // pairs
+    heads = width // HEAD_DIM
     part = rows // groups
     dma = pltpu.SemaphoreType.DMA
     in_hbm = pl.BlockSpec(memory_space=pl.ANY)
@@ -497,19 +562,18 @@
         scratch_shapes=[
             pltpu.VMEM((pairs, rows, features), bf16),
             pltpu.VMEM((pairs, pairs, rows, 2 * shard), bf16),
-            pltpu.VMEM((pairs, 2, shard, 3 * width), bf16),
+            pltpu.VMEM((heads, pairs, 2, shard, 3 * HEAD_DIM), bf16),
             pltpu.VMEM((2, shard, local_width), bf16),
-            pltpu.VMEM((pairs, rows, 3 * width), jnp.float32),
             pltpu.VMEM((pairs, pairs, rows, width), bf16),
             pltpu.VMEM((pairs, rows, 2 * shard), bf16),
             pltpu.VMEM((pairs, groups, part, 2 * shard), bf16),
             pltpu.VMEM((pairs, part, 2 * shard), bf16),
             pltpu.VMEM((pairs, part, 2 * shard), bf16),
-            dma((5,)), dma((pairs,)), dma((pairs,)), dma((pairs,)),
+            dma((2 + 3 * heads,)), dma((pairs,)), dma((pairs,)), dma((pairs,)),
             dma((pairs, groups)), dma((pairs, groups)),
-            dma((pairs, 3)), dma((pairs, 3)), dma((3,)), dma((3,)),
-            dma((pairs,)), dma((pairs,)), dma, dma,
-            dma((pairs, pairs)), dma((pairs, pairs)), dma((pairs, pairs)),
+            dma((pairs, heads, 3)), dma((pairs, heads, 3)), dma((heads, 3)), dma((heads, 3)),
+            dma((pairs, heads)), dma((pairs, heads)), dma, dma,
+            dma((pairs, pairs, heads)), dma((pairs, pairs, heads)), dma((pairs, pairs, heads)),
             dma((pairs, groups)), dma((pairs, groups)), dma((pairs,)), dma((pairs,)),
         ],
         compiler_params=pltpu.CompilerParams(
@@ -528,11 +592,13 @@
     fits = (
         devices % 2 == 0
         and pairs > 1
+        and groups == 4
         and q_w.shape[1] % (pairs * HEAD_DIM) == 0
         and q_w.shape[0] % 128 == 0
         and tokens.shape[0] == IMG_TOKENS
         and tokens.shape[0] % (16 * groups) == 0
         and pairs <= 4
+        and q_w.shape[1] <= 2 * pairs * HEAD_DIM
     )
     if fits:
         return exchanged_heads(pairs, groups, tokens, ln_gain, q_w, k_w, v_w, q_gain, k_gain, out_w)

time: 160 us -> 135 us (0.84); the launches traced: 158 us -> 135 us
  Pallas kernels: 156 us -> 133 us
    pallas_call x1, Pallas kernels: 156 us -> 133 us  [exchanged_heads(): pl.pallas_call(functools.partial(exchange_kernel, pairs, groups), out_sha...]
where the time goes in v2:
time: 135 us
  Pallas kernels  133 us (99%)
  local copies, waits for them, and re-layouts  1.77 us (1%)
    pallas_call x1, Pallas kernels, exchanged_heads(): pl.pallas_call(functools.partial(exchange_kernel, pairs, groups), out_sha...  133 us

profile of v2, /device:TPU:0, one launch (start us, length us, event | category | flops | bytes accessed | tf_op | source)
XLA Modules:
  0.0 135.3 jit_solution(2934768919294080950)
XLA Ops:
  0.0 133.5 %shard_map.82 = bf16[64,3072]{1,0:T(8,128)(2,1)} custom-call(bf16[256,3072]{1,0:T(8,128)(2,1)} %tokens.1, f32[1,3072]{1,0:T(1,128)} %bitcast.3, bf16[384,1024]{1,0:T(8,128)(2,1)} %q_w.1, bf16[384,1024]{1,0:T(8,128)(2,1)} %k_w.1, bf16[384,1024]{1,0:T(8,128)(2,1)} %v_w.1, f32[4,1,256]{2,1,0:T(1,128)} %bitcast.4, f32[4,1,256]{2,1,0:T(1,128)} %bitcast.5, ...), custom_call_target="tpu_custom_call" | custom-call | tf_op jit(solution)/shard_map/pallas_call | solution.py:557
  133.5 1.8 %copy.10 = bf16[64,3072]{1,0:T(8,128)(2,1)} copy(bf16[64,3072]{1,0:T(8,128)(2,1)} %shard_map.82) | data formatting | bytes 786432

commit v3 on v2

--- a/solution.py
+++ b/solution.py
@@ -261,7 +261,6 @@
     for h in range(heads):
         for t in range(3):
             own_weight(h, t).start()
-    out_over().start()
 
     def normalise(block):
         @pl.loop(0, rows // 16)
@@ -320,8 +319,12 @@
         def _():
             cross_tokens(pair + distance)
 
-    send_weights(True, range(1, heads))
-    send_weights(False, range(1, heads))
+        if distance == min(2, pairs - 1):
+            send_weights(True, range(1, heads))
+            send_weights(False, range(1, heads))
+
+
+    out_over().start()
 
     def take_tokens(block):
         from_peer(block, second).wait_recv()

time: 135 us -> 135 us (level)
  no operation moved by 1% of the time
where the time goes in v3:
time: 135 us
  Pallas kernels  133 us (99%)
  local copies, waits for them, and re-layouts  1.77 us (1%)
    pallas_call x1, Pallas kernels, exchanged_heads(): pl.pallas_call(functools.partial(exchange_kernel, pairs, groups), out_sha...  133 us

profile of v3, /device:TPU:0, one launch (start us, length us, event | category | flops | bytes accessed | tf_op | source)
XLA Modules:
  0.0 135.0 jit_solution(3322682897224178310)
XLA Ops:
  0.0 133.2 %shard_map.82 = bf16[64,3072]{1,0:T(8,128)(2,1)} custom-call(bf16[256,3072]{1,0:T(8,128)(2,1)} %tokens.1, f32[1,3072]{1,0:T(1,128)} %bitcast.3, bf16[384,1024]{1,0:T(8,128)(2,1)} %q_w.1, bf16[384,1024]{1,0:T(8,128)(2,1)} %k_w.1, bf16[384,1024]{1,0:T(8,128)(2,1)} %v_w.1, f32[4,1,256]{2,1,0:T(1,128)} %bitcast.4, f32[4,1,256]{2,1,0:T(1,128)} %bitcast.5, ...), custom_call_target="tpu_custom_call" | custom-call | tf_op jit(solution)/shard_map/pallas_call | solution.py:560
  133.2 1.8 %copy.10 = bf16[64,3072]{1,0:T(8,128)(2,1)} copy(bf16[64,3072]{1,0:T(8,128)(2,1)} %shard_map.82) | data formatting | bytes 786432
